TPU v7x, 128 devices: a whole 4x4x4 slice. The times are simulated.
128 devices in a mesh: space: 16 (over y_hi, x, core), code: 4 (over z), clip: 2 (over y_lo).
Axes of the slice: x: 4, y: 4 (y_hi: 2, y_lo: 2; y = y_hi * 2 + y_lo), z: 4, core: 2. Of those that a mesh axis runs over, the one named last changes fastest.
Arguments:
- soft_weights: bfloat16 [2, 1024, 32, 8192], P('clip', 'space', None, 'code'), may hold values from 0.00029945374 to 0.029907227
- codebook: bfloat16 [8192, 256], P('code'), may hold values from -6 to 6
- kernel_one: bfloat16 [3, 3, 256, 512], replicated, may hold values from -0.125 to 0.125
- kernel_two: bfloat16 [3, 3, 512, 512], replicated, may hold values from -0.09375 to 0.09375
- cotangent: bfloat16 [2, 1024, 32, 512], P('clip', ('space', 'code')), may hold values from -16 to 16
Outputs:
- decoded: bfloat16 [2, 1024, 32, 512], P('clip', ('space', 'code'))
- grad_one: float32 [3, 3, 256, 512], P(None, None, None, ('space', 'code', 'clip'))
- grad_two: float32 [3, 3, 512, 512], P(None, None, None, ('space', 'code', 'clip'))
- grad_codebook: float32 [8192, 256], P('code')
All inputs are finite; a program needn't handle non-finite values.
Results may differ from a plain program's by a relative error of at most 0.02.
Values may be sent and summed in bfloat16 or wider, within the bound.
A program may use at most 192 MiB of HBM per device.

v0:
```python
import jax
import jax.numpy as jnp
from jax import lax
from jax.sharding import PartitionSpec as P


def with_halo(block, sides, width):
    for axis, dim in sides:
        count = lax.axis_size(axis)
        forward = [(i, i + 1) for i in range(count - 1)]
        backward = [(target, source) for source, target in forward]
        low = lax.ppermute(
            lax.slice_in_dim(block, block.shape[dim] - width, None, axis=dim), axis, forward
        )
        high = lax.ppermute(lax.slice_in_dim(block, 0, width, axis=dim), axis, backward)
        block = jnp.concatenate([low, block, high], axis=dim)
    return block


def extend(field):
    grown = with_halo(field, ((("space", "code"), 0),), 1)
    return jnp.pad(grown, ((0, 0), (1, 1), (0, 0)))


def taps_forward(padded, kernel):
    height = padded.shape[0] - 2
    breadth = padded.shape[1] - 2
    accum = jnp.zeros((height * breadth, kernel.shape[3]), jnp.float32)
    for first in range(3):
        for second in range(3):
            window = padded[first : first + height, second : second + breadth].reshape(
                height * breadth, -1
            )
            accum = accum + jnp.dot(
                window, kernel[first, second], preferred_element_type=jnp.float32
            )
    return accum.reshape(height, breadth, -1)


def taps_back(padded, kernel):
    height = padded.shape[0] - 2
    breadth = padded.shape[1] - 2
    accum = jnp.zeros((height * breadth, kernel.shape[2]), jnp.float32)
    for first in range(3):
        for second in range(3):
            window = padded[
                2 - first : 2 - first + height, 2 - second : 2 - second + breadth
            ].reshape(height * breadth, -1)
            accum = accum + jnp.dot(
                window, kernel[first, second].T, preferred_element_type=jnp.float32
            )
    return accum.reshape(height, breadth, -1)


def kernel_grad(padded, upstream):
    height = upstream.shape[0]
    breadth = upstream.shape[1]
    flat_up = upstream.reshape(height * breadth, -1)
    result = []
    for first in range(3):
        line = []
        for second in range(3):
            window = padded[first : first + height, second : second + breadth].reshape(
                height * breadth, -1
            )
            line.append(
                lax.dot_general(
                    window, flat_up, (((0,), (0,)), ((), ())), preferred_element_type=jnp.float32
                )
            )
        result.append(jnp.stack(line))
    return jnp.stack(result)


def on_device(soft_weights, codebook, kernel_one, kernel_two, cotangent):
    weights = soft_weights[0]
    upstream = cotangent[0]
    own_rows = upstream.shape[0]
    breadth = weights.shape[1]
    code_slice = weights.shape[2]
    partial_value = jnp.dot(
        weights.reshape(-1, code_slice), codebook, preferred_element_type=jnp.float32
    )
    partial_value = partial_value.reshape(weights.shape[0], breadth, -1)
    summed = lax.psum(partial_value, "code")
    owned = lax.dynamic_slice_in_dim(summed, lax.axis_index("code") * own_rows, own_rows, 0)
    embedded = owned.astype(jnp.bfloat16)
    embed_pad = extend(embedded)
    pre_one = taps_forward(embed_pad, kernel_one)
    hidden = jax.nn.silu(pre_one).astype(jnp.bfloat16)
    hidden_pad = extend(hidden)
    decoded = taps_forward(hidden_pad, kernel_two).astype(jnp.bfloat16)
    grad_hidden = taps_back(extend(upstream), kernel_two)
    sigma = jax.nn.sigmoid(pre_one)
    grad_pre = (grad_hidden * sigma * (1.0 + pre_one * (1.0 - sigma))).astype(jnp.bfloat16)
    grad_embedded = taps_back(extend(grad_pre), kernel_one).astype(jnp.bfloat16)
    piece = lax.all_gather(grad_embedded, "code", axis=0, tiled=True)
    code_terms = lax.dot_general(
        weights.reshape(-1, code_slice),
        piece.reshape(-1, piece.shape[2]),
        (((0,), (0,)), ((), ())),
        preferred_element_type=jnp.float32,
    )
    grad_codebook = lax.psum(code_terms.astype(jnp.bfloat16), ("space", "clip")).astype(jnp.float32)
    term_two = kernel_grad(hidden_pad, upstream)
    term_one = kernel_grad(embed_pad, grad_pre)
    grad_one, grad_two = (
        lax.psum_scatter(term_one, ("space", "code", "clip"), scatter_dimension=3, tiled=True),
        lax.psum_scatter(term_two, ("space", "code", "clip"), scatter_dimension=3, tiled=True),
    )
    return (decoded[None], grad_one, grad_two, grad_codebook)


def solution(mesh):
    in_specs = (
        P("clip", "space", None, "code"),
        P("code", None),
        P(),
        P(),
        P("clip", ("space", "code"), None, None),
    )
    out_specs = (
        P("clip", ("space", "code"), None, None),
        P(None, None, None, ("space", "code", "clip")),
        P(None, None, None, ("space", "code", "clip")),
        P("code", None),
    )
    return jax.shard_map(
        on_device, mesh=mesh, in_specs=in_specs, out_specs=out_specs, check_vma=False
    )
```

profile of v0, /device:TPU:1, one launch (start us, length us, event | category | flops | bytes accessed | tf_op | source)
XLA Modules:
  0.0 509.3 jit_solution(13997313864569233537)
XLA Ops:
  8.4 5.7 %fusion = f32[64,32,256]{2,1,0:T(8,128)S(1)} fusion(bf16[1,64,32,2048]{3,2,1,0:T(8,128)(2,1)} %param.5, bf16[2048,256]{1,0:T(8,128)(2,1)S(1)} %copy-done), kind=kOutput, calls=%fused_computation.1 | convolution fusion | flops 2147483648 | bytes 11534336 | tf_op jit(solution)/shard_map/dot_general | solution.py:81
  14.1 44.1 %all-reduce.14 = bf16[64,32,256]{2,1,0:T(8,128)(2,1)} all-reduce(f32[64,32,256]{2,1,0:T(8,128)S(1)} %fusion), channel_id=1, replica_groups=mesh['space'=16,'code'=4,'clip'=2] {'code'}, use_global_device_ids=true, to_apply=%region_0.0 | all-reduce | flops 524288 | bytes 3145728 | tf_op jit(solution)/shard_map/psum | solution.py:85
  59.4 1.9 collective-permute-start
  61.3 5.2 %collective-permute-start.1 = (bf16[1,32,256]{2,1,0:T(8,128)(2,1)S(1)}, bf16[1,32,256]{2,1,0:T(8,128)(2,1)S(1)}, u32[]{:S(2)}, u32[]{:S(2)}) collective-permute-start(bf16[1,32,256]{2,1,0:T(8,128)(2,1)S(1)} %get-tuple-element.55), channel_id=1, source_target_pairs={{2,0},{4,2},{6,4},{8,6},{10,8},{12,10},{14,12},{16,14},{18,16},{20... | collective-permute-start | bytes 49160 | tf_op jit(solution)/shard_map/ppermute | solution.py:15
  66.5 1.9 collective-permute-start.4
  68.5 4.9 collective-permute-start.5
  76.5 1.5 convolution_bitcast_fusion.4
  88.3 1.9 collective-permute-start.2
  90.2 4.9 collective-permute-start.3
  95.0 1.9 collective-permute-start.6
  97.0 5.0 collective-permute-start.7
  103.2 2.7 pad_maximum_fusion.1
  105.8 7.3 %copy.12 = f32[3,3,256,512]{2,1,0,3:T(4,128)} copy(f32[3,3,256,512]{3,2,1,0:T(8,128)} %pad_maximum_fusion.1) | data formatting | bytes 9437184 | tf_op jit(solution)/shard_map/stack | solution.py:72
  113.4 2.0 fusion.114
  127.8 3.4 maximum_bitcast_fusion
  131.2 27.6 %all-gather.2.cloned.1.call-done = bf16[64,32,256]{2,1,0:T(8,128)(2,1)} async-done(((bf16[16,32,256]{2,1,0:T(8,128)(2,1)}), bf16[64,32,256]{2,1,0:T(8,128)(2,1)}) %all-gather.2.cloned.1.call-update) | async-done | bytes 1048592 | tf_op jit(solution)/shard_map/all_gather | solution.py:97
  158.8 7.0 %fusion.2 = bf16[2048,256]{0,1:T(8,128)(2,1)} fusion(bf16[2048,256]{1,0:T(8,128)(2,1)} %bitcast.297, bf16[2048,2048]{1,0:T(8,128)(2,1)} %bitcast.275), kind=kOutput, calls=%fused_computation.8 | convolution fusion | flops 2148007936 | bytes 10485760 | tf_op jit(solution)/shard_map/dot_general | solution.py:98
  166.1 2.3 maximum_bitcast_fusion.2
  169.9 4.7 pad_maximum_fusion
  174.6 13.8 %copy.13 = f32[3,3,512,512]{2,1,0,3:T(4,128)} copy(f32[3,3,512,512]{3,2,1,0:T(8,128)} %pad_maximum_fusion) | data formatting | bytes 18874368 | tf_op jit(solution)/shard_map/stack | solution.py:72
  188.5 1.7 fusion.32
  190.2 1.5 fusion.14
  191.7 1.5 convolution_add_fusion.13
  193.2 1.5 convolution_add_fusion.12
  194.7 1.6 convolution_add_fusion.11
  196.3 1.5 convolution_add_fusion.10
  197.8 1.5 convolution_add_fusion.9
  199.3 1.5 convolution_add_fusion.8
  200.8 2.4 fusion.7
  203.2 70.1 %all-reduce.11.cloned.1.call-done = bf16[2048,256]{0,1:T(8,128)(2,1)} async-done(((bf16[2048,256]{0,1:T(8,128)(2,1)}), bf16[2048,256]{0,1:T(8,128)(2,1)}) %all-reduce.11.cloned.1.call-update) | async-done | bytes 1048592 | tf_op jit(solution)/shard_map/psum | solution.py:104
  273.2 2.6 copy.16
  275.8 223.9 %all-reduce.13.cloned.1.call-done = (f32[3,3,256,512]{2,1,0,3:T(4,128)}, f32[3,3,512,512]{2,1,0,3:T(4,128)}) async-done(((f32[3,3,256,512]{2,1,0,3:T(4,128)}, f32[3,3,512,512]{2,1,0,3:T(4,128)}), (f32[3,3,256,512]{2,1,0,3:T(4,128)}, f32[3,3,512,512]{2,1,0,3:T(4,128)})) %all-reduce.13.cloned.1.call-update) | async-done | bytes 14155792
  (136 shorter events, 33.8 us)
Async XLA Ops:
  7.2 151.6 %all-gather.2.cloned.1.call-start = ((), (), s32[]{:S(2)}) async-start(), calls=%async_computation | async-start | bytes 1310720 | tf_op jit(solution)/shard_map/all_gather | solution.py:97
  14.1 52.4 %copy-start.2 = (bf16[1,16,32,512]{3,2,1,0:T(8,128)(2,1)S(1)}, bf16[1,16,32,512]{3,2,1,0:T(8,128)(2,1)}, u32[]{:S(2)}) copy-start(bf16[1,16,32,512]{3,2,1,0:T(8,128)(2,1)} %param.9) | copy-start | bytes 1572868
  58.3 15.5 %copy-start.5 = (bf16[3,3,256,512]{3,2,1,0:T(8,128)(2,1)S(1)}, bf16[3,3,256,512]{3,2,1,0:T(8,128)(2,1)}, u32[]{:S(2)}) copy-start(bf16[3,3,256,512]{3,2,1,0:T(8,128)(2,1)} %param.7) | copy-start | bytes 7077892
  59.4 13.9 %collective-permute-start = (bf16[1,32,256]{2,1,0:T(8,128)(2,1)S(1)}, bf16[1,32,256]{2,1,0:T(8,128)(2,1)S(1)}, u32[]{:S(2)}, u32[]{:S(2)}) collective-permute-start(bf16[1,32,256]{2,1,0:T(8,128)(2,1)S(1)} %get-tuple-element.54), channel_id=1, source_target_pairs={{0,2},{2,4},{4,6},{6,8},{8,10},{10,12},{12,14},{14,16},{16,18},{18... | collective-permute-start | bytes 49160 | tf_op jit(solution)/shard_map/ppermute | solution.py:12
  61.3 12.0 %collective-permute-start.1 = (bf16[1,32,256]{2,1,0:T(8,128)(2,1)S(1)}, bf16[1,32,256]{2,1,0:T(8,128)(2,1)S(1)}, u32[]{:S(2)}, u32[]{:S(2)}) collective-permute-start(bf16[1,32,256]{2,1,0:T(8,128)(2,1)S(1)} %get-tuple-element.55), channel_id=1, source_target_pairs={{2,0},{4,2},{6,4},{8,6},{10,8},{12,10},{14,12},{16,14},{18,16},{20... | collective-permute-start | bytes 49160 | tf_op jit(solution)/shard_map/ppermute | solution.py:15
  66.5 11.5 %collective-permute-start.4 = (bf16[1,32,512]{2,1,0:T(8,128)(2,1)S(1)}, bf16[1,32,512]{2,1,0:T(8,128)(2,1)S(1)}, u32[]{:S(2)}, u32[]{:S(2)}) collective-permute-start(bf16[1,32,512]{2,1,0:T(8,128)(2,1)S(1)} %get-tuple-element.40), channel_id=1, source_target_pairs={{0,2},{2,4},{4,6},{6,8},{8,10},{10,12},{12,14},{14,16},{16,18},{18... | collective-permute-start | bytes 98312 | tf_op jit(solution)/shard_map/ppermute | solution.py:12
  68.5 9.6 %collective-permute-start.5 = (bf16[1,32,512]{2,1,0:T(8,128)(2,1)S(1)}, bf16[1,32,512]{2,1,0:T(8,128)(2,1)S(1)}, u32[]{:S(2)}, u32[]{:S(2)}) collective-permute-start(bf16[1,32,512]{2,1,0:T(8,128)(2,1)S(1)} %get-tuple-element.41), channel_id=1, source_target_pairs={{2,0},{4,2},{6,4},{8,6},{10,8},{12,10},{14,12},{16,14},{18,16},{20... | collective-permute-start | bytes 98312 | tf_op jit(solution)/shard_map/ppermute | solution.py:15
  76.5 7.6 %copy-start.19 = (f32[512,512]{1,0:T(8,128)}, f32[512,512]{1,0:T(8,128)S(1)}, u32[]{:S(2)}) copy-start(f32[512,512]{1,0:T(8,128)S(1)} %fusion.6) | copy-start | bytes 3145732
  76.5 2.9 slice-start
  78.0 1.7 slice-start.1
  84.6 3.0 copy-start.6
  84.6 17.8 %copy-start.8 = (bf16[16,32,512]{2,1,0:T(8,128)(2,1)}, bf16[16,32,512]{2,1,0:T(8,128)(2,1)S(1)}, u32[]{:S(2)}) copy-start(bf16[16,32,512]{2,1,0:T(8,128)(2,1)S(1)} %get-tuple-element.14) | copy-start | bytes 1572868
  88.3 24.8 %collective-permute-start.2 = (bf16[1,32,512]{2,1,0:T(8,128)(2,1)}, bf16[1,32,512]{2,1,0:T(8,128)(2,1)S(1)}, u32[]{:S(2)}, u32[]{:S(2)}) collective-permute-start(bf16[1,32,512]{2,1,0:T(8,128)(2,1)} %get-tuple-element.44), channel_id=1, source_target_pairs={{0,2},{2,4},{4,6},{6,8},{8,10},{10,12},{12,14},{14,16},{16,18},{18... | collective-permute-start | bytes 98312 | tf_op jit(solution)/shard_map/ppermute | solution.py:12
  90.2 22.9 %collective-permute-start.3 = (bf16[1,32,512]{2,1,0:T(8,128)(2,1)}, bf16[1,32,512]{2,1,0:T(8,128)(2,1)S(1)}, u32[]{:S(2)}, u32[]{:S(2)}) collective-permute-start(bf16[1,32,512]{2,1,0:T(8,128)(2,1)} %get-tuple-element.45), channel_id=1, source_target_pairs={{2,0},{4,2},{6,4},{8,6},{10,8},{12,10},{14,12},{16,14},{18,16},{20... | collective-permute-start | bytes 98312 | tf_op jit(solution)/shard_map/ppermute | solution.py:15
  95.0 20.3 %collective-permute-start.6 = (bf16[1,32,512]{2,1,0:T(8,128)(2,1)}, bf16[1,32,512]{2,1,0:T(8,128)(2,1)S(1)}, u32[]{:S(2)}, u32[]{:S(2)}) collective-permute-start(bf16[1,32,512]{2,1,0:T(8,128)(2,1)} %get-tuple-element.36), channel_id=1, source_target_pairs={{0,2},{2,4},{4,6},{6,8},{8,10},{10,12},{12,14},{14,16},{16,18},{18... | collective-permute-start | bytes 98312 | tf_op jit(solution)/shard_map/ppermute | solution.py:12
  97.0 18.4 %collective-permute-start.7 = (bf16[1,32,512]{2,1,0:T(8,128)(2,1)}, bf16[1,32,512]{2,1,0:T(8,128)(2,1)S(1)}, u32[]{:S(2)}, u32[]{:S(2)}) collective-permute-start(bf16[1,32,512]{2,1,0:T(8,128)(2,1)} %get-tuple-element.37), channel_id=1, source_target_pairs={{2,0},{4,2},{6,4},{8,6},{10,8},{12,10},{14,12},{16,14},{18,16},{20... | collective-permute-start | bytes 98312 | tf_op jit(solution)/shard_map/ppermute | solution.py:15
  105.8 7.3 %copy-start.7 = (bf16[16,32,512]{2,1,0:T(8,128)(2,1)S(1)}, bf16[16,32,512]{2,1,0:T(8,128)(2,1)}, u32[]{:S(2)}) copy-start(bf16[16,32,512]{2,1,0:T(8,128)(2,1)} %copy-done.6) | copy-start | bytes 1572868
  113.4 2.0 copy-start.9
  120.8 152.5 %all-reduce.11.cloned.1.call-start = ((), (), s32[]{:S(2)}) async-start(), calls=%async_computation.1 | async-start | bytes 2097152 | tf_op jit(solution)/shard_map/psum | solution.py:104
  120.9 2.4 copy-start.17
  120.9 1.9 copy-start.11
  121.4 1.9 copy-start.10
  122.9 1.9 copy-start.12
  123.3 1.9 copy-start.13
  125.7 2.0 copy-start.24
  165.8 333.9 %all-reduce.13.cloned.1.call-start = ((), (), s32[]{:S(2)}) async-start(), calls=%async_computation.2 | async-start | bytes 37748736
  166.1 2.8 copy-start.3
  166.1 3.8 copy-start.4
  188.5 1.7 copy-start.15
  188.5 3.2 copy-start.18
  194.7 1.6 copy-start.21
  200.8 302.0 %copy-start.1 = (bf16[2048,256]{1,0:T(8,128)(2,1)S(1)}, bf16[2048,256]{1,0:T(8,128)(2,1)}, u32[]{:S(2)}) copy-start(bf16[2048,256]{1,0:T(8,128)(2,1)} %param.6) | copy-start | bytes 3145732
  (6 other events, 7.7 us)
Sparse Core Ops, SparseCore 0:
  120.9 37.8 all-gather.1
  166.0 107.2 all-reduce.10
  278.8 220.8 all-reduce.12
where the time goes:
time: 511 us; the launch traced here: 509 us
  waiting for transfers between devices  322 us (63%)
  matrix products  49.1 us (10%)
  blocking collectives  44.1 us (9%)
  local copies, waits for them, and re-layouts  36.6 us (7%)
  starting transfers between devices  27.9 us (5%)
  other arithmetic  15.2 us (3%)
  between operations  14.6 us (3%)
    unnamed x4, waiting for transfers between devices  224 us
    psum x1, waiting for transfers between devices, on_device(): lax.psum(code_terms.astype(jnp.bfloat16), ('space', 'clip'))  70.1 us
    psum x1, blocking collectives, on_device(): summed = lax.psum(partial_value, 'code')  44.1 us
    all_gather x1, waiting for transfers between devices, on_device(): piece = lax.all_gather(grad_embedded, 'code', axis=0, tiled=True)  27.6 us
    another operation x2, local copies, waits for them, and re-layouts, kernel_grad(): return jnp.stack(result)  21.1 us
    ppermute x4, starting transfers between devices, with_halo(): lax.ppermute(lax.slice_in_dim(block, 0, width, axis=dim), axis, backward)  19.9 us
    dot_general x18, matrix products, taps_forward(): jnp.dot(window, kernel[first, second], preferred_element_type=jnp.float32)  17.2 us
    another operation x6, other arithmetic, kernel_grad(): return jnp.stack(result)  13.6 us
  transfers between devices with their start and end apart: 11, of which 3 were waited for; matrix products, arithmetic and copies ran while one was open for 13% of the time, Pallas kernels for 0%

commit v1 on v0

--- a/solution.py
+++ b/solution.py
@@ -94,7 +94,9 @@
     sigma = jax.nn.sigmoid(pre_one)
     grad_pre = (grad_hidden * sigma * (1.0 + pre_one * (1.0 - sigma))).astype(jnp.bfloat16)
     grad_embedded = taps_back(extend(grad_pre), kernel_one).astype(jnp.bfloat16)
-    piece = lax.all_gather(grad_embedded, "code", axis=0, tiled=True)
+    piece = jnp.concatenate(
+        lax.all_to_all(jnp.stack([grad_embedded] * lax.axis_size("code")), "code", 0, 0), axis=0
+    )
     code_terms = lax.dot_general(
         weights.reshape(-1, code_slice),
         piece.reshape(-1, piece.shape[2]),

time: 511 us -> 510 us (level)
  waiting for transfers between devices: 322 us -> 310 us
  starting transfers between devices: 27.9 us -> 34.3 us
    all_gather x1 -> x0, waiting for transfers between devices: 27.6 us -> none  [on_device(): piece = lax.all_gather(grad_embedded, 'code', axis=0, tiled=True)]
    psum x1, waiting for transfers between devices: 70.1 us -> 80.9 us  [on_device(): lax.psum(code_terms.astype(jnp.bfloat16), ('space', 'clip'))]
    all_to_all x0 -> x1, starting transfers between devices: none -> 6.43 us  [on_device(): lax.all_to_all(jnp.stack([grad_embedded] * lax.axis_size('code')), 'code'...]
    unnamed x59 -> x73, local copies, waits for them, and re-layouts: 9.85 us -> 11.2 us
    unnamed x4 -> x3, waiting for transfers between devices: 224 us -> 224 us
where the time goes in v1:
time: 510 us; the launch traced here: 508 us
  waiting for transfers between devices  310 us (61%)
  matrix products  51.2 us (10%)
  blocking collectives  44.1 us (9%)
  local copies, waits for them, and re-layouts  38.5 us (8%)
  starting transfers between devices  34.3 us (7%)
  other arithmetic  15.2 us (3%)
  between operations  14.9 us (3%)
    unnamed x3, waiting for transfers between devices  224 us
    psum x1, waiting for transfers between devices, on_device(): lax.psum(code_terms.astype(jnp.bfloat16), ('space', 'clip'))  80.9 us
    psum x1, blocking collectives, on_device(): summed = lax.psum(partial_value, 'code')  44.1 us
    another operation x2, local copies, waits for them, and re-layouts, kernel_grad(): return jnp.stack(result)  21.1 us
    ppermute x4, starting transfers between devices, with_halo(): lax.ppermute(lax.slice_in_dim(block, 0, width, axis=dim), axis, backward)  19.9 us
    dot_general x18, matrix products, taps_forward(): jnp.dot(window, kernel[first, second], preferred_element_type=jnp.float32)  17.2 us
    dot_general x18, matrix products, kernel_grad(): lax.dot_general(window, flat_up, (((0,), (0,)), ((), ())), preferred_elem...  14 us
    another operation x6, other arithmetic, kernel_grad(): return jnp.stack(result)  13.6 us
  transfers between devices with their start and end apart: 11, of which 3 were waited for; matrix products, arithmetic and copies ran while one was open for 13% of the time, Pallas kernels for 0%

profile of v1, /device:TPU:1, one launch (start us, length us, event | category | flops | bytes accessed | tf_op | source)
XLA Modules:
  0.0 508.1 jit_solution(2508180612318628669)
XLA Ops:
  8.4 5.7 %fusion = f32[64,32,256]{2,1,0:T(8,128)S(1)} fusion(bf16[1,64,32,2048]{3,2,1,0:T(8,128)(2,1)} %param.5, bf16[2048,256]{1,0:T(8,128)(2,1)S(1)} %copy-done), kind=kOutput, calls=%fused_computation.1 | convolution fusion | flops 2147483648 | bytes 11534336 | tf_op jit(solution)/shard_map/dot_general | solution.py:81
  14.1 44.1 %all-reduce.14 = bf16[64,32,256]{2,1,0:T(8,128)(2,1)} all-reduce(f32[64,32,256]{2,1,0:T(8,128)S(1)} %fusion), channel_id=1, replica_groups=mesh['space'=16,'code'=4,'clip'=2] {'code'}, use_global_device_ids=true, to_apply=%region_0.0 | all-reduce | flops 524288 | bytes 3145728 | tf_op jit(solution)/shard_map/psum | solution.py:85
  59.4 1.9 collective-permute-start
  61.3 5.2 %collective-permute-start.1 = (bf16[1,32,256]{2,1,0:T(8,128)(2,1)S(1)}, bf16[1,32,256]{2,1,0:T(8,128)(2,1)S(1)}, u32[]{:S(2)}, u32[]{:S(2)}) collective-permute-start(bf16[1,32,256]{2,1,0:T(8,128)(2,1)S(1)} %get-tuple-element.55), channel_id=1, source_target_pairs={{2,0},{4,2},{6,4},{8,6},{10,8},{12,10},{14,12},{16,14},{18,16},{20... | collective-permute-start | bytes 49160 | tf_op jit(solution)/shard_map/ppermute | solution.py:15
  66.5 1.9 collective-permute-start.4
  68.5 4.9 collective-permute-start.5
  76.5 1.5 convolution_bitcast_fusion.4
  88.3 1.9 collective-permute-start.2
  90.2 4.9 collective-permute-start.3
  95.1 1.9 collective-permute-start.6
  97.0 5.0 collective-permute-start.7
  103.2 2.7 pad_maximum_fusion.1
  105.9 7.3 %copy.12 = f32[3,3,256,512]{2,1,0,3:T(4,128)} copy(f32[3,3,256,512]{3,2,1,0:T(8,128)} %pad_maximum_fusion.1) | data formatting | bytes 9437184 | tf_op jit(solution)/shard_map/stack | solution.py:72
  128.8 6.4 %all-to-all-start = ((bf16[4,16,32,256]{3,2,1,0:T(8,128)(2,1)}), bf16[4,16,32,256]{3,2,1,0:T(8,128)(2,1)S(1)}, u32[]{:S(2)}, u32[]{:S(2)}) async-start(bf16[4,16,32,256]{3,2,1,0:T(8,128)(2,1)} %stack.135), calls=%async_computation | async-start | bytes 2097152 | tf_op jit(solution)/shard_map/all_to_all | solution.py:98
  136.3 1.5 convolution_bitcast_fusion
  138.3 3.4 maximum_bitcast_fusion
  141.7 4.8 all-to-all-done
  146.5 6.7 %fusion.2 = bf16[2048,256]{0,1:T(8,128)(2,1)} fusion(bf16[2048,256]{1,0:T(8,128)(2,1)S(1)} %bitcast.278, bf16[2048,2048]{1,0:T(8,128)(2,1)} %bitcast.275), kind=kOutput, calls=%fused_computation.8 | convolution fusion | flops 2148007936 | bytes 10485760 | tf_op jit(solution)/shard_map/dot_general | solution.py:100
  153.5 2.3 maximum_bitcast_fusion.2
  157.3 4.7 pad_maximum_fusion
  162.0 13.8 %copy.13 = f32[3,3,512,512]{2,1,0,3:T(4,128)} copy(f32[3,3,512,512]{3,2,1,0:T(8,128)} %pad_maximum_fusion) | data formatting | bytes 18874368 | tf_op jit(solution)/shard_map/stack | solution.py:72
  175.8 1.5 fusion.32
  178.9 1.5 convolution_add_fusion.13
  180.4 1.5 convolution_add_fusion.12
  181.9 1.6 convolution_add_fusion.11
  183.5 1.6 convolution_add_fusion.10
  185.1 1.5 convolution_add_fusion.9
  186.7 1.5 convolution_add_fusion.8
  188.2 2.4 fusion.7
  190.6 80.9 %all-reduce.11.cloned.1.call-done = bf16[2048,256]{0,1:T(8,128)(2,1)} async-done(((bf16[2048,256]{0,1:T(8,128)(2,1)}), bf16[2048,256]{0,1:T(8,128)(2,1)}) %all-reduce.11.cloned.1.call-update) | async-done | bytes 1048592 | tf_op jit(solution)/shard_map/psum | solution.py:106
  271.6 2.6 copy.16
  274.1 224.1 %all-reduce.13.cloned.1.call-done = (f32[3,3,256,512]{2,1,0,3:T(4,128)}, f32[3,3,512,512]{2,1,0,3:T(4,128)}) async-done(((f32[3,3,256,512]{2,1,0,3:T(4,128)}, f32[3,3,512,512]{2,1,0,3:T(4,128)}), (f32[3,3,256,512]{2,1,0,3:T(4,128)}, f32[3,3,512,512]{2,1,0,3:T(4,128)})) %all-reduce.13.cloned.1.call-update) | async-done | bytes 14155792
  (150 shorter events, 39.9 us)
Async XLA Ops:
  14.1 52.4 %copy-start.2 = (bf16[1,16,32,512]{3,2,1,0:T(8,128)(2,1)S(1)}, bf16[1,16,32,512]{3,2,1,0:T(8,128)(2,1)}, u32[]{:S(2)}) copy-start(bf16[1,16,32,512]{3,2,1,0:T(8,128)(2,1)} %param.9) | copy-start | bytes 1572868
  58.3 15.5 %copy-start.5 = (bf16[3,3,256,512]{3,2,1,0:T(8,128)(2,1)S(1)}, bf16[3,3,256,512]{3,2,1,0:T(8,128)(2,1)}, u32[]{:S(2)}) copy-start(bf16[3,3,256,512]{3,2,1,0:T(8,128)(2,1)} %param.7) | copy-start | bytes 7077892
  59.4 13.9 %collective-permute-start = (bf16[1,32,256]{2,1,0:T(8,128)(2,1)S(1)}, bf16[1,32,256]{2,1,0:T(8,128)(2,1)S(1)}, u32[]{:S(2)}, u32[]{:S(2)}) collective-permute-start(bf16[1,32,256]{2,1,0:T(8,128)(2,1)S(1)} %get-tuple-element.54), channel_id=1, source_target_pairs={{0,2},{2,4},{4,6},{6,8},{8,10},{10,12},{12,14},{14,16},{16,18},{18... | collective-permute-start | bytes 49160 | tf_op jit(solution)/shard_map/ppermute | solution.py:12
  61.3 12.0 %collective-permute-start.1 = (bf16[1,32,256]{2,1,0:T(8,128)(2,1)S(1)}, bf16[1,32,256]{2,1,0:T(8,128)(2,1)S(1)}, u32[]{:S(2)}, u32[]{:S(2)}) collective-permute-start(bf16[1,32,256]{2,1,0:T(8,128)(2,1)S(1)} %get-tuple-element.55), channel_id=1, source_target_pairs={{2,0},{4,2},{6,4},{8,6},{10,8},{12,10},{14,12},{16,14},{18,16},{20... | collective-permute-start | bytes 49160 | tf_op jit(solution)/shard_map/ppermute | solution.py:15
  66.5 11.5 %collective-permute-start.4 = (bf16[1,32,512]{2,1,0:T(8,128)(2,1)S(1)}, bf16[1,32,512]{2,1,0:T(8,128)(2,1)S(1)}, u32[]{:S(2)}, u32[]{:S(2)}) collective-permute-start(bf16[1,32,512]{2,1,0:T(8,128)(2,1)S(1)} %get-tuple-element.40), channel_id=1, source_target_pairs={{0,2},{2,4},{4,6},{6,8},{8,10},{10,12},{12,14},{14,16},{16,18},{18... | collective-permute-start | bytes 98312 | tf_op jit(solution)/shard_map/ppermute | solution.py:12
  68.5 9.5 %collective-permute-start.5 = (bf16[1,32,512]{2,1,0:T(8,128)(2,1)S(1)}, bf16[1,32,512]{2,1,0:T(8,128)(2,1)S(1)}, u32[]{:S(2)}, u32[]{:S(2)}) collective-permute-start(bf16[1,32,512]{2,1,0:T(8,128)(2,1)S(1)} %get-tuple-element.41), channel_id=1, source_target_pairs={{2,0},{4,2},{6,4},{8,6},{10,8},{12,10},{14,12},{16,14},{18,16},{20... | collective-permute-start | bytes 98312 | tf_op jit(solution)/shard_map/ppermute | solution.py:15
  76.5 7.6 %copy-start.23 = (f32[512,512]{1,0:T(8,128)}, f32[512,512]{1,0:T(8,128)S(1)}, u32[]{:S(2)}) copy-start(f32[512,512]{1,0:T(8,128)S(1)} %fusion.6) | copy-start | bytes 3145732
  76.5 2.9 slice-start
  84.6 3.0 copy-start.8
  84.6 17.9 %copy-start.6 = (bf16[16,32,512]{2,1,0:T(8,128)(2,1)}, bf16[16,32,512]{2,1,0:T(8,128)(2,1)S(1)}, u32[]{:S(2)}) copy-start(bf16[16,32,512]{2,1,0:T(8,128)(2,1)S(1)} %get-tuple-element.14) | copy-start | bytes 1572868
  88.3 24.8 %collective-permute-start.2 = (bf16[1,32,512]{2,1,0:T(8,128)(2,1)}, bf16[1,32,512]{2,1,0:T(8,128)(2,1)S(1)}, u32[]{:S(2)}, u32[]{:S(2)}) collective-permute-start(bf16[1,32,512]{2,1,0:T(8,128)(2,1)} %get-tuple-element.44), channel_id=1, source_target_pairs={{0,2},{2,4},{4,6},{6,8},{8,10},{10,12},{12,14},{14,16},{16,18},{18... | collective-permute-start | bytes 98312 | tf_op jit(solution)/shard_map/ppermute | solution.py:12
  90.2 22.9 %collective-permute-start.3 = (bf16[1,32,512]{2,1,0:T(8,128)(2,1)}, bf16[1,32,512]{2,1,0:T(8,128)(2,1)S(1)}, u32[]{:S(2)}, u32[]{:S(2)}) collective-permute-start(bf16[1,32,512]{2,1,0:T(8,128)(2,1)} %get-tuple-element.45), channel_id=1, source_target_pairs={{2,0},{4,2},{6,4},{8,6},{10,8},{12,10},{14,12},{16,14},{18,16},{20... | collective-permute-start | bytes 98312 | tf_op jit(solution)/shard_map/ppermute | solution.py:15
  95.1 27.9 %collective-permute-start.6 = (bf16[1,32,512]{2,1,0:T(8,128)(2,1)}, bf16[1,32,512]{2,1,0:T(8,128)(2,1)S(1)}, u32[]{:S(2)}, u32[]{:S(2)}) collective-permute-start(bf16[1,32,512]{2,1,0:T(8,128)(2,1)} %get-tuple-element.36), channel_id=1, source_target_pairs={{0,2},{2,4},{4,6},{6,8},{8,10},{10,12},{12,14},{14,16},{16,18},{18... | collective-permute-start | bytes 98312 | tf_op jit(solution)/shard_map/ppermute | solution.py:12
  97.0 26.0 %collective-permute-start.7 = (bf16[1,32,512]{2,1,0:T(8,128)(2,1)}, bf16[1,32,512]{2,1,0:T(8,128)(2,1)S(1)}, u32[]{:S(2)}, u32[]{:S(2)}) collective-permute-start(bf16[1,32,512]{2,1,0:T(8,128)(2,1)} %get-tuple-element.37), channel_id=1, source_target_pairs={{2,0},{4,2},{6,4},{8,6},{10,8},{12,10},{14,12},{16,14},{18,16},{20... | collective-permute-start | bytes 98312 | tf_op jit(solution)/shard_map/ppermute | solution.py:15
  105.9 7.3 %copy-start.9 = (bf16[16,32,512]{2,1,0:T(8,128)(2,1)S(1)}, bf16[16,32,512]{2,1,0:T(8,128)(2,1)}, u32[]{:S(2)}) copy-start(bf16[16,32,512]{2,1,0:T(8,128)(2,1)} %copy-done.8) | copy-start | bytes 1572868
  113.2 2.9 copy-start.12
  117.8 5.1 %copy-start.14 = (bf16[16,32,512]{2,1,0:T(8,128)(2,1)}, bf16[16,32,512]{2,1,0:T(8,128)(2,1)S(1)}, u32[]{:S(2)}) copy-start(bf16[16,32,512]{2,1,0:T(8,128)(2,1)S(1)} %get-tuple-element.28) | copy-start | bytes 1572868
  117.8 5.2 %copy-start.18 = (bf16[16,32,512]{2,1,0:T(8,128)(2,1)}, bf16[16,32,512]{2,1,0:T(8,128)(2,1)S(1)}, u32[]{:S(2)}) copy-start(bf16[16,32,512]{2,1,0:T(8,128)(2,1)S(1)} %get-tuple-element.30) | copy-start | bytes 1572868
  120.1 2.9 copy-start.7
  127.4 7.9 %copy-start.20 = (bf16[16,32,512]{2,1,0:T(8,128)(2,1)S(1)}, bf16[16,32,512]{2,1,0:T(8,128)(2,1)}, u32[]{:S(2)}) copy-start(bf16[16,32,512]{2,1,0:T(8,128)(2,1)} %get-tuple-element.31) | copy-start | bytes 1572868
  128.8 6.9 %copy-start.22 = (bf16[16,32,512]{2,1,0:T(8,128)(2,1)S(1)}, bf16[16,32,512]{2,1,0:T(8,128)(2,1)}, u32[]{:S(2)}) copy-start(bf16[16,32,512]{2,1,0:T(8,128)(2,1)} %get-tuple-element.32) | copy-start | bytes 1572868
  128.8 17.6 %all-to-all-start = ((bf16[4,16,32,256]{3,2,1,0:T(8,128)(2,1)}), bf16[4,16,32,256]{3,2,1,0:T(8,128)(2,1)S(1)}, u32[]{:S(2)}, u32[]{:S(2)}) async-start(bf16[4,16,32,256]{3,2,1,0:T(8,128)(2,1)} %stack.135), calls=%async_computation | async-start | bytes 2097152 | tf_op jit(solution)/shard_map/all_to_all | solution.py:98
  135.3 136.3 %all-reduce.11.cloned.1.call-start = ((), (), s32[]{:S(2)}) async-start(), calls=%async_computation.1 | async-start | bytes 2097152 | tf_op jit(solution)/shard_map/psum | solution.py:106
  135.7 2.1 copy-start.26
  135.7 2.1 copy-start.27
  135.7 2.1 copy-start.28
  135.8 2.6 copy-start.31
  153.2 345.0 %all-reduce.13.cloned.1.call-start = ((), (), s32[]{:S(2)}) async-start(), calls=%async_computation.2 | async-start | bytes 37748736
  153.5 2.8 copy-start.3
  153.5 3.8 copy-start.4
  175.8 3.0 copy-start.13
  188.2 313.0 %copy-start.1 = (bf16[2048,256]{1,0:T(8,128)(2,1)S(1)}, bf16[2048,256]{1,0:T(8,128)(2,1)}, u32[]{:S(2)}) copy-start(bf16[2048,256]{1,0:T(8,128)(2,1)} %param.6) | copy-start | bytes 3145732
  (13 other events, 18.5 us)
Sparse Core Ops, SparseCore 0:
  153.3 118.1 all-reduce.10
  277.1 221.0 all-reduce.12
